TPU v7x, 32 devices: a whole 2x2x4 slice. The times are simulated.
32 devices in a mesh: grp: 2 (over x), gx: 4 (over z), gy: 4 (over y, core).
Axes of the slice: x: 2, y: 2, z: 4, core: 2. Of those that a mesh axis runs over, the one named last changes fastest.
Arguments:
- theta_anomaly: float32 [192, 64, 128], P(('grp', 'gx'), 'gy'), may hold values from -4 to 4
- humidity_ratio: float32 [192, 64, 128], P(('grp', 'gx'), 'gy'), may hold values from 0.6 to 1.4
- zonal_velocity: float32 [192, 64, 128], P(('grp', 'gx'), 'gy'), may hold values from -1.8 to 1.8
- meridional_velocity: float32 [192, 64, 128], P(('grp', 'gx'), 'gy'), may hold values from -1.8 to 1.8
- vertical_velocity: float32 [192, 64, 128], P(('grp', 'gx'), 'gy'), may hold values from -1.8 to 1.8
- patch_processor_map: int32 [8, 4, 8], P(('grp', 'gx'), 'gy'), may hold values from 0 to 3, as said below
- particle_bucket_population: int32 [8, 4, 8], P(('grp', 'gx'), 'gy'), may hold values from 0 to 1024, as said below
- particle_size_quadratic: float32 [8, 4, 8, 1024], P(('grp', 'gx'), 'gy'), may hold values from 0.25 to 4
- represented_number: float32 [8, 4, 8, 1024], P(('grp', 'gx'), 'gy'), may hold values from 0.5 to 2
- particle_location_number: int32 [8, 4, 8, 1024], P(('grp', 'gx'), 'gy'), may hold values from 48 to 6095, as said below
Outputs:
- final_temperature: float32 [192, 64, 128], P(('grp', 'gx'), 'gy')
- final_vapour: float32 [192, 64, 128], P(('grp', 'gx'), 'gy')
- final_east: float32 [192, 64, 128], P(('grp', 'gx'), 'gy')
- final_north: float32 [192, 64, 128], P(('grp', 'gx'), 'gy')
- final_vertical: float32 [192, 64, 128], P(('grp', 'gx'), 'gy')
- final_size_quadratic: float32 [8, 4, 8, 1024], P(('grp', 'gx'), 'gy')
Inputs may be any that keep to these rules, and one draw needn't show every extreme that they name: `patch_processor_map`: entry [a, y, b] is the index along gx of the device in the same row (same grp half, same gy) that holds the droplets of column block b of device (a, y). Different blocks of one device go to different owners, so one device sends at most 2 blocks to one owner; in every row some owner holds 2 blocks from every device of the row. `particle_bucket_population`: entry [a, y, r] counts the live droplets of slot r = s x 2 + t of the owner (a, y); they are the first ones of the slot. A slot that receives no block has none; every slot of an owner that holds 2 blocks from every device is full. `particle_location_number`: the cell within the slot's block, column 128 + level, with levels from 48 to 79. Within a slot the live droplets are sorted by column, and so are the others.
All inputs are finite; a program needn't handle non-finite values.
Results may differ from a plain program's by a relative error of at most 0.0003.
Values sent between devices are 32-bit elements; how exact they have to be, the bound alone decides.
A program may use at most 64 MiB of HBM per device.

v0:
```python
import jax
import jax.numpy as jnp
from jax import lax
from jax.sharding import PartitionSpec as P

NBD = 8
NSUB = 4
ITERS = 4


TIME_INCREMENT = 0.15
THERMAL_LIFT = 0.5
HUMID_LIFT = 0.3
HELMHOLTZ = 0.001
CLAUSIUS_FACTOR = 0.2
GROWTH = 0.5
GROWTH_SLOPE = 0.1
SUB_STEP = 0.25
CURVATURE = 0.05
FLOOR_SQUARE = 0.04
CONDENSE = 0.2
PHASE_WARMING = 2.5


def with_halo(block, sides, width):
    for axis, dim in sides:
        count = lax.axis_size(axis)
        forward = [(i, i + 1) for i in range(count - 1)]
        forward.append((count - 1, 0))
        backward = [(target, source) for source, target in forward]
        low = lax.ppermute(
            lax.slice_in_dim(block, block.shape[dim] - width, None, axis=dim), axis, forward
        )
        high = lax.ppermute(lax.slice_in_dim(block, 0, width, axis=dim), axis, backward)
        block = jnp.concatenate([low, block, high], axis=dim)
    return block


def surround(stacked):
    return with_halo(stacked, ((("grp", "gx"), 1), ("gy", 2)), 1)


def beside(padded):
    return (
        padded[:, 2:, 1:-1, :],
        padded[:, :-2, 1:-1, :],
        padded[:, 1:-1, 2:, :],
        padded[:, 1:-1, :-2, :],
    )


def level_above(values):
    return jnp.concatenate([values[..., 1:], jnp.zeros_like(values[..., :1])], axis=-1)


def level_below(values):
    return jnp.concatenate([jnp.zeros_like(values[..., :1]), values[..., :-1]], axis=-1)


def profiles(layer_altitudes):
    heights = jnp.arange(layer_altitudes, dtype=jnp.float32)
    midpoint_mass_per_volume = jnp.exp(-(heights + 0.5) / layer_altitudes)
    interface_mass_per_volume = jnp.where(
        heights < layer_altitudes - 1, jnp.exp(-(heights + 1.0) / layer_altitudes), 0.0
    )
    return (midpoint_mass_per_volume, interface_mass_per_volume)


def operate(values, midpoint_mass_per_volume, interface_mass_per_volume):
    east_side, west_side, north_side, south_side = beside(surround(values[None]))
    return (
        midpoint_mass_per_volume
        * ((4.0 + HELMHOLTZ) * values - east_side[0] - west_side[0] - north_side[0] - south_side[0])
        + interface_mass_per_volume * (values - level_above(values))
        + level_below(interface_mass_per_volume) * (values - level_below(values))
    )


def both_sums(residual, applied):
    return lax.psum(
        (jnp.sum(residual * residual), jnp.sum(residual * applied)), ("grp", "gx", "gy")
    )


def solve_pressure(right_side, midpoint_mass_per_volume, interface_mass_per_volume):
    potential = jnp.zeros_like(right_side)
    residual = right_side
    applied = operate(residual, midpoint_mass_per_volume, interface_mass_per_volume)
    norm_now, product = both_sums(residual, applied)
    step_length = norm_now / product
    direction, along_dir = (residual, applied)
    for iteration in range(ITERS):
        potential = potential + step_length * direction
        residual = residual - step_length * along_dir
        if iteration + 1 < ITERS:
            applied = operate(residual, midpoint_mass_per_volume, interface_mass_per_volume)
            norm_next, product = both_sums(residual, applied)
            beta_ratio = norm_next / norm_now
            step_length = norm_next / (product - beta_ratio * norm_next / step_length)
            direction = residual + beta_ratio * direction
            along_dir = applied + beta_ratio * along_dir
            norm_now = norm_next
    return potential


def momentum_update(
    theta_anomaly,
    humidity_ratio,
    zonal_velocity,
    meridional_velocity,
    vertical_velocity,
    midpoint_mass_per_volume,
    interface_mass_per_volume,
):
    raised_airmass = vertical_velocity + TIME_INCREMENT * (
        THERMAL_LIFT * theta_anomaly + HUMID_LIFT * humidity_ratio
    )
    east_side, west_side, north_side, south_side = beside(
        surround(jnp.stack([zonal_velocity, meridional_velocity]))
    )
    divergence = midpoint_mass_per_volume * (
        (east_side[0] - west_side[0]) * 0.5 + (north_side[1] - south_side[1]) * 0.5
    ) + 0.5 * (
        level_above(midpoint_mass_per_volume * raised_airmass)
        - level_below(midpoint_mass_per_volume * raised_airmass)
    )
    potential = solve_pressure(
        -divergence / TIME_INCREMENT, midpoint_mass_per_volume, interface_mass_per_volume
    )
    pot_east, pot_west, pot_north, pot_south = beside(surround(potential[None]))
    zonal_velocity = zonal_velocity - TIME_INCREMENT * 0.5 * (pot_east[0] - pot_west[0])
    meridional_velocity = meridional_velocity - TIME_INCREMENT * 0.5 * (pot_north[0] - pot_south[0])
    vertical_velocity = raised_airmass - TIME_INCREMENT * 0.5 * (
        level_above(potential) - level_below(potential)
    )
    scalar_quantities = jnp.stack([theta_anomaly, humidity_ratio])
    tra_east, tra_west, tra_north, tra_south = beside(surround(scalar_quantities))
    lower_level = jnp.concatenate(
        [scalar_quantities[..., :1], scalar_quantities[..., :-1]], axis=-1
    )
    upper_level = jnp.concatenate(
        [scalar_quantities[..., 1:], scalar_quantities[..., -1:]], axis=-1
    )
    tendency = (
        jnp.maximum(zonal_velocity, 0.0) * (scalar_quantities - tra_west)
        + jnp.minimum(zonal_velocity, 0.0) * (tra_east - scalar_quantities)
        + jnp.maximum(meridional_velocity, 0.0) * (scalar_quantities - tra_south)
        + jnp.minimum(meridional_velocity, 0.0) * (tra_north - scalar_quantities)
        + jnp.maximum(vertical_velocity, 0.0) * (scalar_quantities - lower_level)
        + jnp.minimum(vertical_velocity, 0.0) * (upper_level - scalar_quantities)
    )
    moved = scalar_quantities - TIME_INCREMENT * tendency
    return (moved[0], moved[1], zonal_velocity, meridional_velocity, vertical_velocity)


def grow_droplets(supersat_ratio, warmth, particle_size_quadratic, represented_number, alive_mask):
    growth_rate = GROWTH * jnp.exp(GROWTH_SLOPE * warmth)
    square_now = particle_size_quadratic
    for substep in range(NSUB):
        square_now = jnp.maximum(
            square_now
            + 2.0 * SUB_STEP * growth_rate * (supersat_ratio - CURVATURE / jnp.sqrt(square_now)),
            FLOOR_SQUARE,
        )
    grown_square = jnp.where(alive_mask, square_now, particle_size_quadratic)
    mass_change = jnp.where(
        alive_mask,
        represented_number
        * (
            grown_square * jnp.sqrt(grown_square)
            - particle_size_quadratic * jnp.sqrt(particle_size_quadratic)
        ),
        0.0,
    )
    return (grown_square, mass_change)


def grow_rows(columns, radius_squared_rows, mult_rows, local_cell, alive_mask):
    row_count = columns.shape[0]
    thermal_couple = columns.reshape(row_count, 2, -1)
    cells_per = thermal_couple.shape[2]
    supersat_ratio = jnp.take_along_axis(thermal_couple[:, 0], local_cell, axis=1)
    warmth = jnp.take_along_axis(thermal_couple[:, 1], local_cell, axis=1)
    grown_square, mass_change = grow_droplets(
        supersat_ratio, warmth, radius_squared_rows, mult_rows, alive_mask
    )
    flat_cell = local_cell + cells_per * jnp.arange(row_count, dtype=jnp.int32)[:, None]
    liquid_content = CONDENSE * jax.ops.segment_sum(
        mass_change.reshape(-1), flat_cell.reshape(-1), num_segments=row_count * cells_per
    )
    return (grown_square, liquid_content.reshape(row_count, cells_per))


def into_patches(values):
    domain_length_east, domain_length_north, layer_depth = values.shape
    shaped = values.reshape(domain_length_east, NBD, domain_length_north // NBD, layer_depth)
    return shaped.transpose(1, 0, 2, 3).reshape(NBD, -1)


def from_blocks(blocks, domain_length_east, domain_length_north, layer_depth):
    shaped = blocks.reshape(NBD, domain_length_east, domain_length_north // NBD, layer_depth)
    return shaped.transpose(1, 0, 2, 3).reshape(
        domain_length_east, domain_length_north, layer_depth
    )


def routing_plan(owner_row, slots, row_count):
    row_index = jnp.arange(row_count, dtype=jnp.int32)[:, None]
    block_index = jnp.arange(owner_row.shape[0], dtype=jnp.int32)[None, :]
    matches = (owner_row[None, :] == row_index // slots) & (
        block_index % slots == row_index % slots
    )
    return matches.astype(jnp.float32)


def on_device(
    theta_anomaly,
    humidity_ratio,
    zonal_velocity,
    meridional_velocity,
    vertical_velocity,
    patch_processor_map,
    particle_bucket_population,
    particle_size_quadratic,
    represented_number,
    particle_location_number,
):
    domain_length_east, domain_length_north, layer_altitudes = theta_anomaly.shape
    midpoint_mass_per_volume, interface_mass_per_volume = profiles(layer_altitudes)
    radius_squared_rows = particle_size_quadratic[0, 0]
    mult_rows = represented_number[0, 0]
    cell_rows = particle_location_number[0, 0]
    count_rows = particle_bucket_population[0, 0]
    row_count = radius_squared_rows.shape[0]
    slots = row_count // lax.axis_size("gx")
    routing = routing_plan(patch_processor_map[0, 0], slots, row_count)
    layer_low = 0
    layer_depth = layer_altitudes - layer_low
    local_cell = (
        cell_rows // layer_altitudes * layer_depth + cell_rows % layer_altitudes - layer_low
    )
    alive_mask = (
        jnp.arange(radius_squared_rows.shape[1], dtype=jnp.int32)[None, :] < count_rows[:, None]
    )
    advected_theta, advected_humidity, zonal_velocity, meridional_velocity, vertical_velocity = (
        momentum_update(
            theta_anomaly,
            humidity_ratio,
            zonal_velocity,
            meridional_velocity,
            vertical_velocity,
            midpoint_mass_per_volume,
            interface_mass_per_volume,
        )
    )
    supersat_ratio = advected_humidity * jnp.exp(-CLAUSIUS_FACTOR * advected_theta) - 1.0
    thermal_couple = jnp.stack(
        [into_patches(supersat_ratio), into_patches(advected_theta)], axis=1
    ).reshape(NBD, -1)
    columns = jnp.dot(routing, thermal_couple, precision=lax.Precision.HIGHEST)
    arrived_columns = lax.all_to_all(columns, "gx", split_axis=0, concat_axis=0, tiled=True)
    radius_squared_rows, owner_rows = grow_rows(
        arrived_columns, radius_squared_rows, mult_rows, local_cell, alive_mask
    )
    condensed_rows = lax.all_to_all(owner_rows, "gx", split_axis=0, concat_axis=0, tiled=True)
    liquid_content = from_blocks(
        jnp.dot(routing.T, condensed_rows, precision=lax.Precision.HIGHEST),
        domain_length_east,
        domain_length_north,
        layer_depth,
    )
    theta_anomaly = advected_theta + PHASE_WARMING * liquid_content
    humidity_ratio = advected_humidity - liquid_content
    return (
        theta_anomaly,
        humidity_ratio,
        zonal_velocity,
        meridional_velocity,
        vertical_velocity,
        radius_squared_rows[None, None],
    )


def solution(mesh):
    placed = (
        P(("grp", "gx"), "gy", None),
        P(("grp", "gx"), "gy", None),
        P(("grp", "gx"), "gy", None),
        P(("grp", "gx"), "gy", None),
        P(("grp", "gx"), "gy", None),
        P(("grp", "gx"), "gy", None),
        P(("grp", "gx"), "gy", None),
        P(("grp", "gx"), "gy", None, None),
        P(("grp", "gx"), "gy", None, None),
        P(("grp", "gx"), "gy", None, None),
    )
    return jax.shard_map(
        on_device,
        mesh=mesh,
        in_specs=placed,
        out_specs=(
            P(("grp", "gx"), "gy", None),
            P(("grp", "gx"), "gy", None),
            P(("grp", "gx"), "gy", None),
            P(("grp", "gx"), "gy", None),
            P(("grp", "gx"), "gy", None),
            P(("grp", "gx"), "gy", None, None),
        ),
        check_vma=False,
    )
```

profile of v0, /device:TPU:0, one launch (start us, length us, event | category | flops | bytes accessed | tf_op | source)
XLA Modules:
  0.0 446.6 jit_solution(3342073956511347936)
XLA Ops:
  0.7 0.8 pad_maximum_fusion.74
  1.5 6.0 %collective-permute-start = (f32[2,1,16,128]{3,2,1,0:T(8,128)S(1)}, f32[2,1,16,128]{3,2,1,0:T(8,128)S(1)}, u32[]{:S(2)}, u32[]{:S(2)}) collective-permute-start(f32[2,1,16,128]{3,2,1,0:T(8,128)S(1)} %get-tuple-element.59), channel_id=1, source_target_pairs={{4,0},{8,4},{12,8},{16,12},{20,16},{24,20},{28,24},{0,28},{5,1},{9... | collective-permute-start | bytes 49160 | tf_op jit(solution)/shard_map/ppermute | solution.py:34
  8.3 4.7 %collective-permute-start.23 = (f32[2,1,16,128]{3,1,2,0:T(1,128)}, f32[2,1,16,128]{3,1,2,0:T(1,128)}, u32[]{:S(2)}, u32[]{:S(2)}) collective-permute-start(f32[2,1,16,128]{3,1,2,0:T(1,128)} %get-tuple-element.65), channel_id=1, source_target_pairs={{4,0},{8,4},{12,8},{16,12},{20,16},{24,20},{28,24},{0,28},{5,1},{9... | collective-permute-start | bytes 49160 | tf_op jit(solution)/shard_map/ppermute | solution.py:34
  15.1 1.1 collective-permute-done.2
  16.2 2.0 collective-permute-done.3
  18.4 2.0 collective-permute-start.4
  20.5 1.5 collective-permute-done.4
  22.1 4.7 %collective-permute-done.5 = f32[1,1,16,128]{3,2,1,0:T(8,128)S(1)} collective-permute-done((f32[1,1,16,128]{3,2,1,0:T(8,128)S(1)}, f32[1,1,16,128]{3,2,1,0:T(8,128)S(1)}, u32[]{:S(2)}, u32[]{:S(2)}) %collective-permute-start.5) | collective-permute-done | bytes 8224 | tf_op jit(solution)/shard_map/ppermute | solution.py:31
  27.5 0.8 collective-permute-done.6
  28.3 1.8 collective-permute-done.7
  30.0 0.8 multiply_reduce_fusion.5
  30.8 37.1 %all-reduce.15 = (f32[]{:T(128)}, f32[]{:T(128)}) all-reduce(f32[]{:T(128)} %get-tuple-element.26, f32[]{:T(128)} %get-tuple-element.25), channel_id=1, replica_groups=mesh['grp'=2,'gx'=4,'gy'=4] {'grp','gx','gy'}, use_global_device_ids=true, to_apply=%region_1.2 | all-reduce | flops 2 | bytes 16 | tf_op jit(solution)/shard_map/psum | solution.py:80
  69.3 4.0 collective-permute-start.8
  73.5 1.2 collective-permute-done.8
  74.7 5.0 %collective-permute-done.9 = f32[1,1,16,128]{3,2,1,0:T(8,128)S(1)} collective-permute-done((f32[1,1,16,128]{3,2,1,0:T(8,128)S(1)}, f32[1,1,16,128]{3,2,1,0:T(8,128)S(1)}, u32[]{:S(2)}, u32[]{:S(2)}) %collective-permute-start.9) | collective-permute-done | bytes 8224 | tf_op jit(solution)/shard_map/ppermute | solution.py:31
  80.4 0.8 collective-permute-done.10
  81.2 1.9 collective-permute-done.11
  83.8 37.2 %all-reduce.14 = (f32[]{:T(128)}, f32[]{:T(128)}) all-reduce(f32[]{:T(128)} %get-tuple-element.24, f32[]{:T(128)} %get-tuple-element.23), channel_id=1, replica_groups=mesh['grp'=2,'gx'=4,'gy'=4] {'grp','gx','gy'}, use_global_device_ids=true, to_apply=%region_5.6 | all-reduce | flops 2 | bytes 16 | tf_op jit(solution)/shard_map/psum | solution.py:80
  125.7 4.0 collective-permute-start.12
  129.7 0.9 fusion.2
  131.9 4.2 collective-permute-done.13
  136.8 0.8 collective-permute-done.14
  137.6 1.9 collective-permute-done.15
  139.5 1.5 multiply_reduce_fusion.1
  141.0 37.2 %all-reduce.13 = (f32[]{:T(128)}, f32[]{:T(128)}) all-reduce(f32[]{:T(128)} %get-tuple-element.22, f32[]{:T(128)} %get-tuple-element.21), channel_id=1, replica_groups=mesh['grp'=2,'gx'=4,'gy'=4] {'grp','gx','gy'}, use_global_device_ids=true, to_apply=%region_9.10 | all-reduce | flops 2 | bytes 16 | tf_op jit(solution)/shard_map/psum | solution.py:80
  182.0 1.0 multiply_subtract_fusion.1
  183.0 4.0 collective-permute-start.16
  187.0 1.3 pad_maximum_fusion.69
  188.4 1.7 collective-permute-start.27
  190.1 3.3 collective-permute-done.17
  194.9 2.2 collective-permute-done.19
  197.2 0.8 fusion.37
  197.9 37.4 %all-reduce.12 = (f32[]{:T(128)}, f32[]{:T(128)}) all-reduce(f32[]{:T(128)} %get-tuple-element.20, f32[]{:T(128)} %get-tuple-element.19), channel_id=1, replica_groups=mesh['grp'=2,'gx'=4,'gy'=4] {'grp','gx','gy'}, use_global_device_ids=true, to_apply=%region_13.14 | all-reduce | flops 2 | bytes 16 | tf_op jit(solution)/shard_map/psum | solution.py:80
  239.5 4.0 collective-permute-start.20
  243.6 1.2 collective-permute-done.20
  244.8 5.0 %collective-permute-done.21 = f32[1,1,16,128]{3,2,1,0:T(8,128)S(1)} collective-permute-done((f32[1,1,16,128]{3,2,1,0:T(8,128)S(1)}, f32[1,1,16,128]{3,2,1,0:T(8,128)S(1)}, u32[]{:S(2)}, u32[]{:S(2)}) %collective-permute-start.21) | collective-permute-done | bytes 8224 | tf_op jit(solution)/shard_map/ppermute | solution.py:31
  251.3 1.9 collective-permute-done.25
  254.4 0.8 copy-done.4
  255.2 1.2 fusion.10
  257.4 1.3 fusion.110
  258.6 3.8 all-to-all-start
  262.8 11.6 %all-to-all-done = f32[4,2,12288]{2,1,0:T(2,128)S(1)} async-done(((f32[4,2,12288]{2,1,0:T(2,128)}), f32[4,2,12288]{2,1,0:T(2,128)S(1)}, u32[]{:S(2)}, u32[]{:S(2)}) %all-to-all-start) | async-done | bytes 393248 | tf_op jit(solution)/shard_map/all_to_all | solution.py:261
  275.3 50.0 %gather_fusion = f32[8192]{0:T(1024)S(1)} fusion(f32[8,6144]{1,0:T(8,128)S(1)} %bitcast.262, s32[8192]{0:T(1024)S(1)} %bitcast.263), kind=kCustom, calls=%fused_computation.clone | custom fusion | bytes 131072 | tf_op jit(solution)/shard_map/jit(take_along_axis)/gather | solution.py:183
  325.5 50.0 %gather_fusion.1 = f32[8192]{0:T(1024)S(1)} fusion(f32[8,6144]{1,0:T(8,128)S(1)} %bitcast.261, s32[8192]{0:T(1024)S(1)} %bitcast.264), kind=kCustom, calls=%fused_computation.1.clone | custom fusion | bytes 131072 | tf_op jit(solution)/shard_map/jit(take_along_axis)/gather | solution.py:182
  376.3 56.7 %scatter_custom_fusion = f32[49152]{0:T(1024)S(1)} fusion(s32[8192]{0:T(1024)S(1)} %bitcast.293, f32[8192]{0:T(1024)S(1)} %bitcast.294, f32[]{:T(128)} %constant.107.clone.1), kind=kCustom, calls=%fused_computation.191 | custom fusion | flops 8192 | bytes 196612 | tf_op jit(solution)/shard_map/scatter-add | solution.py:188
  433.1 0.8 all_to_all.13
  433.9 3.5 all-to-all-start.1
  437.4 7.3 %all-to-all-done.1 = f32[4,2,6144]{2,1,0:T(2,128)S(1)} async-done(((f32[4,2,6144]{2,1,0:T(2,128)}), f32[4,2,6144]{2,1,0:T(2,128)S(1)}, u32[]{:S(2)}, u32[]{:S(2)}) %all-to-all-start.1) | async-done | bytes 196640 | tf_op jit(solution)/shard_map/all_to_all | solution.py:265
  (165 shorter events, 16.7 us)
Async XLA Ops:
  0.6 6.8 %copy-start.3 = (f32[24,16,128]{2,1,0:T(8,128)S(1)}, f32[24,16,128]{2,1,0:T(8,128)}, u32[]{:S(2)}) copy-start(f32[24,16,128]{2,1,0:T(8,128)} %param.12) | copy-start | bytes 589828
  0.6 6.8 %copy-start.2 = (f32[24,16,128]{2,1,0:T(8,128)S(1)}, f32[24,16,128]{2,1,0:T(8,128)}, u32[]{:S(2)}) copy-start(f32[24,16,128]{2,1,0:T(8,128)} %param.13) | copy-start | bytes 589828
  1.5 13.0 %collective-permute-start = (f32[2,1,16,128]{3,2,1,0:T(8,128)S(1)}, f32[2,1,16,128]{3,2,1,0:T(8,128)S(1)}, u32[]{:S(2)}, u32[]{:S(2)}) collective-permute-start(f32[2,1,16,128]{3,2,1,0:T(8,128)S(1)} %get-tuple-element.59), channel_id=1, source_target_pairs={{4,0},{8,4},{12,8},{16,12},{20,16},{24,20},{28,24},{0,28},{5,1},{9... | collective-permute-start | bytes 49160 | tf_op jit(solution)/shard_map/ppermute | solution.py:34
  7.5 7.0 %collective-permute-start.1 = (f32[2,1,16,128]{3,2,1,0:T(8,128)S(1)}, f32[2,1,16,128]{3,2,1,0:T(8,128)S(1)}, u32[]{:S(2)}, u32[]{:S(2)}) collective-permute-start(f32[2,1,16,128]{3,2,1,0:T(8,128)S(1)} %get-tuple-element.58), channel_id=1, source_target_pairs={{0,4},{4,8},{8,12},{12,16},{16,20},{20,24},{24,28},{28,0},{1,5},{5... | collective-permute-start | bytes 49160 | tf_op jit(solution)/shard_map/ppermute | solution.py:31
  7.6 5.4 %copy-start.6 = (f32[24,16,128]{2,1,0:T(8,128)S(1)}, f32[24,16,128]{2,1,0:T(8,128)}, u32[]{:S(2)}) copy-start(f32[24,16,128]{2,1,0:T(8,128)} %param.16) | copy-start | bytes 589828
  8.2 178.8 %collective-permute-start.22 = (f32[2,1,16,128]{3,1,2,0:T(1,128)}, f32[2,1,16,128]{3,1,2,0:T(1,128)S(1)}, u32[]{:S(2)}, u32[]{:S(2)}) collective-permute-start(f32[2,1,16,128]{3,1,2,0:T(1,128)} %get-tuple-element.64), channel_id=1, source_target_pairs={{0,4},{4,8},{8,12},{12,16},{16,20},{20,24},{24,28},{28,0},{1,5},{5... | collective-permute-start | bytes 49160 | tf_op jit(solution)/shard_map/ppermute | solution.py:31
  8.3 178.8 %collective-permute-start.23 = (f32[2,1,16,128]{3,1,2,0:T(1,128)}, f32[2,1,16,128]{3,1,2,0:T(1,128)}, u32[]{:S(2)}, u32[]{:S(2)}) collective-permute-start(f32[2,1,16,128]{3,1,2,0:T(1,128)} %get-tuple-element.65), channel_id=1, source_target_pairs={{4,0},{8,4},{12,8},{16,12},{20,16},{24,20},{28,24},{0,28},{5,1},{9... | collective-permute-start | bytes 49160 | tf_op jit(solution)/shard_map/ppermute | solution.py:34
  13.0 126.5 %copy-start.20 = (f32[128]{0:T(128)}, f32[128]{0:T(128)S(1)}, u32[]{:S(2)}) copy-start(f32[128]{0:T(128)S(1)} %multiply_exponential_fusion) | copy-start | bytes 1540
  14.5 1.7 collective-permute-start.2
  14.7 3.5 collective-permute-start.3
  15.1 124.4 %copy-start.23 = (f32[128]{0:T(128)}, f32[128]{0:T(128)S(1)}, u32[]{:S(2)}) copy-start(f32[128]{0:T(128)S(1)} %compare_select_fusion.4) | copy-start | bytes 1540
  18.4 3.7 collective-permute-start.4
  20.4 6.3 %collective-permute-start.5 = (f32[1,1,16,128]{3,2,1,0:T(8,128)S(1)}, f32[1,1,16,128]{3,2,1,0:T(8,128)S(1)}, u32[]{:S(2)}, u32[]{:S(2)}) collective-permute-start(f32[1,1,16,128]{3,2,1,0:T(8,128)S(1)} %get-tuple-element.94), channel_id=1, source_target_pairs={{0,4},{4,8},{8,12},{12,16},{16,20},{20,24},{24,28},{28,0},{1,5},{5... | collective-permute-start | bytes 24584 | tf_op jit(solution)/shard_map/ppermute | solution.py:31
  20.5 118.9 %copy-start.25 = (f32[128]{0:T(128)}, f32[128]{0:T(128)S(1)}, u32[]{:S(2)}) copy-start(f32[128]{0:T(128)S(1)} %pad_maximum_fusion.91) | copy-start | bytes 1540
  26.8 1.5 collective-permute-start.6
  26.9 3.2 collective-permute-start.7
  69.3 5.4 %collective-permute-start.8 = (f32[1,1,16,128]{3,2,1,0:T(8,128)S(1)}, f32[1,1,16,128]{3,2,1,0:T(8,128)S(1)}, u32[]{:S(2)}, u32[]{:S(2)}) collective-permute-start(f32[1,1,16,128]{3,2,1,0:T(8,128)S(1)} %get-tuple-element.91), channel_id=1, source_target_pairs={{4,0},{8,4},{12,8},{16,12},{20,16},{24,20},{28,24},{0,28},{5,1},{9... | collective-permute-start | bytes 24584 | tf_op jit(solution)/shard_map/ppermute | solution.py:34
  73.3 6.3 %collective-permute-start.9 = (f32[1,1,16,128]{3,2,1,0:T(8,128)S(1)}, f32[1,1,16,128]{3,2,1,0:T(8,128)S(1)}, u32[]{:S(2)}, u32[]{:S(2)}) collective-permute-start(f32[1,1,16,128]{3,2,1,0:T(8,128)S(1)} %get-tuple-element.90), channel_id=1, source_target_pairs={{0,4},{4,8},{8,12},{12,16},{16,20},{20,24},{24,28},{28,0},{1,5},{5... | collective-permute-start | bytes 24584 | tf_op jit(solution)/shard_map/ppermute | solution.py:31
  79.7 1.5 collective-permute-start.10
  79.8 3.3 collective-permute-start.11
  125.7 6.2 %collective-permute-start.12 = (f32[1,1,16,128]{3,2,1,0:T(8,128)S(1)}, f32[1,1,16,128]{3,2,1,0:T(8,128)S(1)}, u32[]{:S(2)}, u32[]{:S(2)}) collective-permute-start(f32[1,1,16,128]{3,2,1,0:T(8,128)S(1)} %get-tuple-element.87), channel_id=1, source_target_pairs={{4,0},{8,4},{12,8},{16,12},{20,16},{24,20},{28,24},{0,28},{5,1},{9... | collective-permute-start | bytes 24584 | tf_op jit(solution)/shard_map/ppermute | solution.py:34
  129.7 6.3 %collective-permute-start.13 = (f32[1,1,16,128]{3,2,1,0:T(8,128)S(1)}, f32[1,1,16,128]{3,2,1,0:T(8,128)S(1)}, u32[]{:S(2)}, u32[]{:S(2)}) collective-permute-start(f32[1,1,16,128]{3,2,1,0:T(8,128)S(1)} %get-tuple-element.86), channel_id=1, source_target_pairs={{0,4},{4,8},{8,12},{12,16},{16,20},{20,24},{24,28},{28,0},{1,5},{5... | collective-permute-start | bytes 24584 | tf_op jit(solution)/shard_map/ppermute | solution.py:31
  136.1 1.5 collective-permute-start.14
  136.2 3.3 collective-permute-start.15
  183.0 7.1 %collective-permute-start.16 = (f32[1,1,16,128]{3,2,1,0:T(8,128)S(1)}, f32[1,1,16,128]{3,2,1,0:T(8,128)S(1)}, u32[]{:S(2)}, u32[]{:S(2)}) collective-permute-start(f32[1,1,16,128]{3,2,1,0:T(8,128)S(1)} %get-tuple-element.85), channel_id=1, source_target_pairs={{4,0},{8,4},{12,8},{16,12},{20,16},{24,20},{28,24},{0,28},{5,1},{9... | collective-permute-start | bytes 24584 | tf_op jit(solution)/shard_map/ppermute | solution.py:34
  187.0 6.3 %collective-permute-start.17 = (f32[1,1,16,128]{3,2,1,0:T(8,128)S(1)}, f32[1,1,16,128]{3,2,1,0:T(8,128)S(1)}, u32[]{:S(2)}, u32[]{:S(2)}) collective-permute-start(f32[1,1,16,128]{3,2,1,0:T(8,128)S(1)} %get-tuple-element.84), channel_id=1, source_target_pairs={{0,4},{4,8},{8,12},{12,16},{16,20},{20,24},{24,28},{28,0},{1,5},{5... | collective-permute-start | bytes 24584 | tf_op jit(solution)/shard_map/ppermute | solution.py:31
  188.3 66.0 %collective-permute-start.26 = (f32[2,26,1,128]{3,1,2,0:T(8,128)}, f32[2,26,1,128]{3,1,2,0:T(8,128)}, u32[]{:S(2)}, u32[]{:S(2)}) collective-permute-start(f32[2,26,1,128]{3,1,2,0:T(8,128)} %get-tuple-element.52), channel_id=1, source_target_pairs={{0,1},{1,2},{2,3},{3,0},{4,5},{5,6},{6,7},{7,4},{8,9},{9,10},{10,1... | collective-permute-start | bytes 79880 | tf_op jit(solution)/shard_map/ppermute | solution.py:31
  188.4 66.0 %collective-permute-start.27 = (f32[2,26,1,128]{3,1,2,0:T(8,128)}, f32[2,26,1,128]{3,1,2,0:T(8,128)}, u32[]{:S(2)}, u32[]{:S(2)}) collective-permute-start(f32[2,26,1,128]{3,1,2,0:T(8,128)} %get-tuple-element.53), channel_id=1, source_target_pairs={{1,0},{2,1},{3,2},{0,3},{5,4},{6,5},{7,6},{4,7},{9,8},{10,9},{11,1... | collective-permute-start | bytes 79880 | tf_op jit(solution)/shard_map/ppermute | solution.py:34
  190.1 3.4 copy-start.16
  193.4 1.5 collective-permute-start.18
  194.0 3.1 copy-start.26
  194.0 3.1 collective-permute-start.19
  239.3 4.2 copy-start.7
  239.5 5.4 %collective-permute-start.20 = (f32[1,1,16,128]{3,2,1,0:T(8,128)S(1)}, f32[1,1,16,128]{3,2,1,0:T(8,128)S(1)}, u32[]{:S(2)}, u32[]{:S(2)}) collective-permute-start(f32[1,1,16,128]{3,2,1,0:T(8,128)S(1)} %get-tuple-element.79), channel_id=1, source_target_pairs={{4,0},{8,4},{12,8},{16,12},{20,16},{24,20},{28,24},{0,28},{5,1},{9... | collective-permute-start | bytes 24584 | tf_op jit(solution)/shard_map/ppermute | solution.py:34
  243.5 6.3 %collective-permute-start.21 = (f32[1,1,16,128]{3,2,1,0:T(8,128)S(1)}, f32[1,1,16,128]{3,2,1,0:T(8,128)S(1)}, u32[]{:S(2)}, u32[]{:S(2)}) collective-permute-start(f32[1,1,16,128]{3,2,1,0:T(8,128)S(1)} %get-tuple-element.78), channel_id=1, source_target_pairs={{0,4},{4,8},{8,12},{12,16},{16,20},{20,24},{24,28},{28,0},{1,5},{5... | collective-permute-start | bytes 24584 | tf_op jit(solution)/shard_map/ppermute | solution.py:31
  243.6 6.9 %copy-start.5 = (f32[24,16,128]{2,1,0:T(8,128)}, f32[24,16,128]{2,1,0:T(8,128)S(1)}, u32[]{:S(2)}) copy-start(f32[24,16,128]{2,1,0:T(8,128)S(1)} %get-tuple-element.42) | copy-start | bytes 589828
  249.8 1.5 collective-permute-start.24
  249.9 3.3 collective-permute-start.25
  258.6 3.8 copy-start.12
  258.6 3.8 copy-start.13
  258.6 4.1 copy-start.11
  258.6 15.8 %all-to-all-start = ((f32[4,2,12288]{2,1,0:T(2,128)}), f32[4,2,12288]{2,1,0:T(2,128)S(1)}, u32[]{:S(2)}, u32[]{:S(2)}) async-start(f32[4,2,12288]{2,1,0:T(2,128)} %fusion.110), calls=%async_computation | async-start | bytes 786432 | tf_op jit(solution)/shard_map/all_to_all | solution.py:261
  325.4 50.1 %copy-start.14 = (f32[1,1,8,1024]{3,2,1,0:T(8,128)S(1)}, f32[1,1,8,1024]{3,2,1,0:T(8,128)}, u32[]{:S(2)}) copy-start(f32[1,1,8,1024]{3,2,1,0:T(8,128)} %param.19) | copy-start | bytes 98308
  325.5 50.1 %copy-start.15 = (f32[1,1,8,1024]{3,2,1,0:T(8,128)S(1)}, f32[1,1,8,1024]{3,2,1,0:T(8,128)}, u32[]{:S(2)}) copy-start(f32[1,1,8,1024]{3,2,1,0:T(8,128)} %param.20) | copy-start | bytes 98308
  325.5 50.1 %copy-start.31 = (s32[1,1,8]{2,1,0:T(1,128)S(1)}, s32[1,1,8]{2,1,0:T(1,128)}, u32[]{:S(2)}) copy-start(s32[1,1,8]{2,1,0:T(1,128)} %param.18) | copy-start | bytes 100
  433.9 10.9 %copy-start.28 = (s32[8]{0:T(128)S(1)}, s32[8]{0:T(128)}, u32[]{:S(2)}) copy-start(s32[8]{0:T(128)} %copy-done.27) | copy-start | bytes 100
  433.9 10.9 %copy-start.30 = (s32[1,1,8]{2,1,0:T(1,128)S(1)}, s32[1,1,8]{2,1,0:T(1,128)}, u32[]{:S(2)}) copy-start(s32[1,1,8]{2,1,0:T(1,128)} %param.17) | copy-start | bytes 100
  433.9 10.8 %all-to-all-start.1 = ((f32[4,2,6144]{2,1,0:T(2,128)}), f32[4,2,6144]{2,1,0:T(2,128)S(1)}, u32[]{:S(2)}, u32[]{:S(2)}) async-start(f32[4,2,6144]{2,1,0:T(2,128)} %all_to_all.13), calls=%async_computation.1 | async-start | bytes 393216 | tf_op jit(solution)/shard_map/all_to_all | solution.py:265
  (14 other events, 21.5 us)
where the time goes:
time: 448 us; the launch traced here: 447 us
  blocking collectives  149 us (33%)
  local copies, waits for them, and re-layouts  109 us (24%)
  other arithmetic  69.3 us (15%)
  waiting for transfers between devices  61.6 us (14%)
  starting transfers between devices  40.9 us (9%)
  between operations  15.2 us (3%)
    psum x4, blocking collectives, both_sums(): lax.psum((jnp.sum(residual * residual), jnp.sum(residual * applied)), ('g...  149 us
    scatter-add x1, other arithmetic, grow_rows(): jax.ops.segment_sum(mass_change.reshape(-1), flat_cell.reshape(-1), num_s...  56.7 us
    gather x2, local copies, waits for them, and re-layouts, grow_rows(): warmth = jnp.take_along_axis(thermal_couple[:, 1], local_cell, axis=1)  50.1 us
    gather x2, local copies, waits for them, and re-layouts, grow_rows(): jnp.take_along_axis(thermal_couple[:, 0], local_cell, axis=1)  50.1 us
    ppermute x14, waiting for transfers between devices, with_halo(): lax.ppermute(lax.slice_in_dim(block, block.shape[dim] - width, None, axis...  33.7 us
    ppermute x14, starting transfers between devices, with_halo(): lax.ppermute(lax.slice_in_dim(block, 0, width, axis=dim), axis, backward)  31.1 us
    all_to_all x1, waiting for transfers between devices, on_device(): lax.all_to_all(columns, 'gx', split_axis=0, concat_axis=0, tiled=True)  11.6 us
  transfers between devices with their start and end apart: 30, of which 22 were waited for; matrix products, arithmetic and copies ran while one was open for 3% of the time, Pallas kernels for 0%

commit v1 on v0

v1 whole, which is shorter than its diff:
```python
import functools

import jax
import jax.numpy as jnp
from jax import lax
from jax.experimental import pallas as pl
from jax.experimental.pallas import tpu as pltpu
from jax.sharding import PartitionSpec as P

NBD = 8
NSUB = 4
ITERS = 4
KLO = 48
KHI = 80

DT = 0.15
THERMAL_LIFT = 0.5
HUMID_LIFT = 0.3
HELMHOLTZ = 0.001
CLAUSIUS_FACTOR = 0.2
GROWTH = 0.5
GROWTH_SLOPE = 0.1
SUB_STEP = 0.25
CURVATURE = 0.05
FLOOR_SQUARE = 0.04
CONDENSE = 0.2
PHASE_WARMING = 2.5

H = 5
HY = 8
MESH = pl.DeviceIdType.MESH
HIGH = lax.Precision.HIGHEST


def cg_coefficients(m):
    def inner(a, b):
        total = None
        for i, ai in enumerate(a):
            part = None
            for j, bj in enumerate(b):
                term = bj * (0.5 * (m[i + j] + m[abs(i - j)]))
                part = term if part is None else part + term
            part = ai * part
            total = part if total is None else total + part
        return total

    one = jnp.ones_like(m[0])
    zero = jnp.zeros_like(m[0])

    def apply(d):
        out = [zero] * (len(d) + 1)
        for i, di in enumerate(d):
            out[i] = out[i] + 6.0 * di
            if i == 0:
                out[1] = out[1] + 6.0 * di
            else:
                out[i + 1] = out[i + 1] + 3.0 * di
                out[i - 1] = out[i - 1] + 3.0 * di
        return out

    res, d, pot, rr = [one], [one], [], m[0]
    for it in range(ITERS):
        img = apply(d)
        alpha = rr / inner(d, img)
        pot = [
            alpha * d[i] + (pot[i] if i < len(pot) else 0.0) for i in range(len(d))
        ]
        if it + 1 == ITERS:
            break
        res = [(res[i] if i < len(res) else zero) - alpha * img[i] for i in range(len(img))]
        new = inner(res, res)
        beta = new / rr
        d = [res[i] + (beta * d[i] if i < len(d) else 0.0) for i in range(len(res))]
        rr = new
    return pot


def kernel(
    ngrp, ngx, ngy, slots,
    t_ref, q_ref, u_ref, v_ref, w_ref, map_ref, cnt_ref, size_ref, mult_ref, cell_ref,
    to_ref, qo_ref, uo_ref, vo_ref, wo_ref, so_ref,
    ue, ve, le, te, qe, p0, p1, p2, p3, pack, got, part, got_x, part2, got_y,
    blk, out1, in1, sat_s, tmp_s, out2, in2, cond, grid_c, packed,
    send_sem, recv_sem,
):
    cx, cy, nz = t_ref.shape
    rows = 2 * HY + cy
    grp, gx, gy = lax.axis_index("grp"), lax.axis_index("gx"), lax.axis_index("gy")
    nx = ngrp * ngx
    xt = grp * ngx + gx

    def dev(dx, dy):
        other = lax.rem(xt + dx + nx, nx)
        return (lax.div(other, ngx), lax.rem(other, ngx), lax.rem(gy + dy + ngy, ngy))

    barrier = pltpu.get_barrier_semaphore()
    greet = [dev(o, 0) for o in range(1, nx)] + [dev(0, o) for o in range(1, ngy)]
    greet += [dev(a, b) for a in (-1, 1) for b in (-1, 1)]
    greet += []
    for target in greet:
        pl.semaphore_signal(barrier, inc=1, device_id=target, device_id_type=MESH)

    own = slice(HY, HY + cy)

    def stage(x, c):
        tt, qq, uu, vv = t_ref[x], q_ref[x], u_ref[x], v_ref[x]
        lift = w_ref[x] + DT * (THERMAL_LIFT * tt + HUMID_LIFT * qq)
        ue[x + H, own, :] = uu
        ve[x + H, own, :] = vv
        le[x + H, own, :] = lift
        te[x + H, own, :] = tt
        qe[x + H, own, :] = qq
        pack[0, x, 0:4, :] = uu[cy - 4 :]
        pack[0, x, 4:9, :] = vv[cy - 5 :]
        pack[0, x, 9:13, :] = lift[cy - 4 :]
        pack[0, x, 13:14, :] = tt[cy - 1 :]
        pack[0, x, 14:15, :] = qq[cy - 1 :]
        pack[1, x, 0:4, :] = uu[0:4]
        pack[1, x, 4:9, :] = vv[0:5]
        pack[1, x, 9:13, :] = lift[0:4]
        pack[1, x, 13:14, :] = tt[0:1]
        pack[1, x, 14:15, :] = qq[0:1]
        return c

    lax.fori_loop(0, cx, stage, 0)
    pl.semaphore_wait(barrier, len(greet))

    sems = [0]
    started = []

    def send(src, dst, target):
        i = sems[0]
        sems[0] += 1
        copy = pltpu.make_async_remote_copy(
            src_ref=src, dst_ref=dst, send_sem=send_sem.at[i], recv_sem=recv_sem.at[i],
            device_id=target, device_id_type=MESH,
        )
        copy.start()
        started.append(copy)
        return copy

    e = H + cx
    halo = []
    east, west = dev(1, 0), dev(-1, 0)
    halo.append(send(u_ref.at[pl.ds(cx - 5, 5)], ue.at[pl.ds(0, 5), own], east))
    halo.append(send(u_ref.at[pl.ds(0, 5)], ue.at[pl.ds(e, 5), own], west))
    halo.append(send(v_ref.at[pl.ds(cx - 4, 4)], ve.at[pl.ds(1, 4), own], east))
    halo.append(send(v_ref.at[pl.ds(0, 4)], ve.at[pl.ds(e, 4), own], west))
    halo.append(send(le.at[pl.ds(e - 4, 4), own], le.at[pl.ds(1, 4), own], east))
    halo.append(send(le.at[pl.ds(H, 4), own], le.at[pl.ds(e, 4), own], west))
    halo.append(send(pack.at[0], got.at[0, pl.ds(H, cx)], dev(0, 1)))
    halo.append(send(pack.at[1], got.at[1, pl.ds(H, cx)], dev(0, -1)))
    for a, dy in ((0, 1), (1, -1)):
        halo.append(send(pack.at[a, pl.ds(cx - 5, 5)], got.at[a, pl.ds(0, 5)], dev(1, dy)))
        halo.append(send(pack.at[a, pl.ds(0, 5)], got.at[a, pl.ds(e, 5)], dev(-1, dy)))
    for src, dst in ((t_ref, te), (q_ref, qe)):
        halo.append(send(src.at[pl.ds(cx - 1, 1)], dst.at[pl.ds(H - 1, 1), own], east))
        halo.append(send(src.at[pl.ds(0, 1)], dst.at[pl.ds(e, 1), own], west))

    lane = lax.broadcasted_iota(jnp.int32, (1, nz), 1)
    height = lane.astype(jnp.float32)
    rho = jnp.exp(-(height + 0.5) / nz)
    face = jnp.where(lane < nz - 1, jnp.exp(-(height + 1.0) / nz), 0.0)
    face_dn = jnp.where(lane > 0, jnp.exp(-height / nz), 0.0)
    not_top = jnp.where(lane < nz - 1, 1.0, 0.0)
    not_bot = jnp.where(lane > 0, 1.0, 0.0)
    rho_up = jnp.where(lane < nz - 1, jnp.exp(-(height + 1.5) / nz), 0.0)
    rho_dn = jnp.where(lane > 0, jnp.exp(-(height - 0.5) / nz), 0.0)

    def up(f):
        return pltpu.roll(f, nz - 1, 1)

    def down(f):
        return pltpu.roll(f, 1, 1)

    for copy in halo:
        copy.wait_recv()

    def unpack(x, c):
        s, n = got[0, x], got[1, x]
        ue[x, HY - 4 : HY, :] = s[0:4]
        ve[x, HY - 5 : HY, :] = s[4:9]
        le[x, HY - 4 : HY, :] = s[9:13]
        te[x, HY - 1 : HY, :] = s[13:14]
        qe[x, HY - 1 : HY, :] = s[14:15]
        ue[x, HY + cy : HY + cy + 4, :] = n[0:4]
        ve[x, HY + cy : HY + cy + 5, :] = n[4:9]
        le[x, HY + cy : HY + cy + 4, :] = n[9:13]
        te[x, HY + cy : HY + cy + 1, :] = n[13:14]
        qe[x, HY + cy : HY + cy + 1, :] = n[14:15]
        return c

    lax.fori_loop(0, cx + 2 * H, unpack, 0)

    def make_r(x, c):
        vv, ll = ve[x], le[x]
        horiz = (ue[x + 1] - ue[x - 1]) + (pltpu.roll(vv, rows - 1, 0) - pltpu.roll(vv, 1, 0))
        div = rho * (0.5 * horiz) + 0.5 * (rho_up * up(ll) - rho_dn * down(ll))
        p0[x] = div * (-1.0 / DT)
        return c

    lax.fori_loop(1, cx + 2 * H - 1, make_r, 0)

    diag = ((4.0 + HELMHOLTZ) * rho + face + face_dn) / 6.0 - 1.0
    rho6, face6, face_dn6 = rho / 6.0, face / 6.0, face_dn / 6.0

    def scaled(f, x):
        c = f[x]
        side = f[x + 1] + f[x - 1] + pltpu.roll(c, rows - 1, 0) + pltpu.roll(c, 1, 0)
        return diag * c - rho6 * side - face6 * up(c) - face_dn6 * down(c)

    def step1(x, c):
        p1[x] = scaled(p0, x)
        return c

    def step2(x, c):
        p2[x] = 2.0 * scaled(p1, x) - p0[x]
        return c

    def step3(x, c):
        p3[x] = 2.0 * scaled(p2, x) - p1[x]
        return c

    full = cx + 2 * H
    lax.fori_loop(2, full - 2, step1, 0)
    lax.fori_loop(3, full - 3, step2, 0)
    lax.fori_loop(4, full - 4, step3, 0)

    def dots(x, acc):
        a0, a1, a2, a3 = p0[x, own, :], p1[x, own, :], p2[x, own, :], p3[x, own, :]
        side = p3[x + 1, own, :] + p3[x - 1, own, :]
        side = side + p3[x, HY - 1 : HY + cy - 1, :] + p3[x, HY + 1 : HY + cy + 1, :]
        a4 = 2.0 * (diag * a3 - rho6 * side - face6 * up(a3) - face_dn6 * down(a3)) - a2
        pairs = ((a0, a0), (a0, a1), (a1, a1), (a1, a2), (a2, a2), (a2, a3), (a3, a3), (a3, a4))
        return tuple(s + f * g for s, (f, g) in zip(acc, pairs))

    acc = lax.fori_loop(H, e, dots, (jnp.zeros((cy, nz), jnp.float32),) * 8)
    for i in range(8):
        part[i : i + 1, :] = jnp.sum(acc[i], axis=0, keepdims=True)

    peers = [send(part, got_x.at[o - 1], dev(o, 0)) for o in range(1, nx)]
    total = part[...]
    for o, copy in enumerate(peers):
        copy.wait_recv()
        total = total + got_x[o]
    part2[...] = total
    peers = [send(part2, got_y.at[o - 1], dev(0, o)) for o in range(1, ngy)]
    for o, copy in enumerate(peers):
        copy.wait_recv()
        total = total + got_y[o]
    total = jnp.broadcast_to(jnp.sum(total, axis=1, keepdims=True), (8, nz))
    dot = [total[i : i + 1, :] for i in range(8)]
    m = [dot[0], dot[1]]
    for k in range(2, 8):
        m.append(2.0 * dot[k] - m[k % 2])
    c0, c1, c2, c3 = cg_coefficients(m)

    def potential(x, c):
        p0[x] = c0 * p0[x] + c1 * p1[x] + c2 * p2[x] + c3 * p3[x]
        return c

    lax.fori_loop(H - 1, e + 1, potential, 0)

    sub = lax.broadcasted_iota(jnp.int32, (cy, nz), 0)
    lanes = lax.broadcasted_iota(jnp.int32, (cy, nz), 1)
    nlev = KHI - KLO
    half = 2 * nlev
    south = slice(HY - 1, HY + cy - 1)
    north = slice(HY + 1, HY + cy + 1)

    def advance(x, c):
        g = x + H
        phi = p0[g, own, :]
        u = ue[g, own, :] - (DT * 0.5) * (p0[g + 1, own, :] - p0[g - 1, own, :])
        v = ve[g, own, :] - (DT * 0.5) * (p0[g, north, :] - p0[g, south, :])
        w = le[g, own, :] - (DT * 0.5) * (not_top * up(phi) - not_bot * down(phi))
        uo_ref[x] = u
        vo_ref[x] = v
        wo_ref[x] = w
        u_p, u_m = jnp.maximum(u, 0.0), jnp.minimum(u, 0.0)
        v_p, v_m = jnp.maximum(v, 0.0), jnp.minimum(v, 0.0)
        w_p, w_m = jnp.maximum(w, 0.0) * not_bot, jnp.minimum(w, 0.0) * not_top

        def move(f):
            h = f[g, own, :]
            return h - DT * (
                u_p * (h - f[g - 1, own, :])
                + u_m * (f[g + 1, own, :] - h)
                + v_p * (h - f[g, south, :])
                + v_m * (f[g, north, :] - h)
                + w_p * (h - down(h))
                + w_m * (up(h) - h)
            )

        tt, qq = move(te), move(qe)
        to_ref[x] = tt
        qo_ref[x] = qq
        sat = qq * jnp.exp(-CLAUSIUS_FACTOR * tt) - 1.0
        both = jnp.where(
            lanes < nlev, pltpu.roll(sat, nz - KLO, 1), pltpu.roll(tt, nz - KLO + nlev, 1)
        )
        odd = pltpu.roll(pltpu.roll(both, cy - 1, 0), half, 1)
        packed[x] = jnp.where(lanes < half, both, odd)
        return c

    lax.fori_loop(0, cx, advance, 0)
    for x in range(cx):
        for b in range(NBD):
            blk[b, x : x + 1, :] = packed[x, 2 * b : 2 * b + 1, :]

    nrow = ngx * slots
    for r in range(nrow):
        o, t = r // slots, r % slots
        row = None
        for b in range(t, NBD, slots):
            term = jnp.where(map_ref[0, b] == o, 1.0, 0.0) * blk[b]
            row = term if row is None else row + term
        out1[r] = row

    def exchange(src, dst):
        copies = []
        for o in range(1, ngx):
            other = lax.rem(gx + o, ngx)
            copies.append(
                send(
                    src.at[pl.ds(other * slots, slots)],
                    dst.at[pl.ds(gx * slots, slots)],
                    (grp, other, gy),
                )
            )
        for t in range(slots):
            dst[gx * slots + t] = src[gx * slots + t]
        for copy in copies:
            copy.wait_recv()

    exchange(out1, in1)

    dpb = size_ref.shape[1]
    wide = lax.broadcasted_iota(jnp.int32, (nz, dpb), 0)
    narrow = lax.broadcasted_iota(jnp.int32, (cx, dpb), 0)

    def place(r):
        cell = cell_ref[pl.ds(r, 1), :]
        lx = cell // (2 * nz)
        s = (cell // nz) % 2 * half + cell % nz - KLO
        return jnp.where(narrow == lx, 1.0, 0.0), s

    for r in range(nrow):
        hot, s = place(r)
        res = lax.dot_general(
            in1[r], hot, (((0,), (0,)), ((), ())), precision=HIGH,
            preferred_element_type=jnp.float32,
        )
        sat_s[r : r + 1, :] = jnp.sum(jnp.where(wide == s, res, 0.0), axis=0, keepdims=True)
        tmp_s[r : r + 1, :] = jnp.sum(
            jnp.where(wide == s + nlev, res, 0.0), axis=0, keepdims=True
        )

    rate = (2.0 * SUB_STEP * GROWTH) * jnp.exp(GROWTH_SLOPE * tmp_s[...])
    gain = rate * sat_s[...]
    loss = rate * CURVATURE
    old = size_ref[...]
    x2 = old
    for _ in range(NSUB):
        x2 = jnp.maximum(x2 + gain - loss * lax.rsqrt(x2), FLOOR_SQUARE)
    alive = lax.broadcasted_iota(jnp.int32, (nrow, dpb), 1) < cnt_ref[...]
    new = jnp.where(alive, x2, old)
    so_ref[...] = new
    sat_s[...] = jnp.where(
        alive,
        CONDENSE * mult_ref[...] * (new * jnp.sqrt(new) - old * jnp.sqrt(old)),
        0.0,
    )

    for r in range(nrow):
        hot, s = place(r)
        mass = jnp.where(wide == s, sat_s[r : r + 1, :], 0.0)
        out2[r] = lax.dot_general(
            hot, mass, (((1,), (1,)), ((), ())), precision=HIGH,
            preferred_element_type=jnp.float32,
        )

    exchange(out2, in2)

    for b in range(NBD):
        acc = None
        for o in range(ngx):
            term = jnp.where(map_ref[0, b] == o, 1.0, 0.0) * in2[o * slots + b % slots]
            acc = term if acc is None else acc + term
        cond[b] = acc
    for x in range(cx):
        for b in range(NBD):
            line = cond[b, x : x + 1, :]
            grid_c[x, 2 * b : 2 * b + 1, :] = line
            grid_c[x, 2 * b + 1 : 2 * b + 2, :] = line

    even = sub % 2 == 0
    inside = (lanes >= KLO) & (lanes < KHI)

    def finish(x, c):
        f = grid_c[x]
        f = jnp.where(even, pltpu.roll(f, KLO, 1), pltpu.roll(f, nz + KLO - half, 1))
        f = jnp.where(inside, f, 0.0)
        to_ref[x] = to_ref[x] + PHASE_WARMING * f
        qo_ref[x] = qo_ref[x] - f
        return c

    lax.fori_loop(0, cx, finish, 0)
    for copy in started:
        copy.wait_send()


def on_device(ngrp, ngx, ngy, t, q, u, v, w, owner, count, size, mult, cell):
    cx, cy, nz = t.shape
    nrow, dpb = size.shape[2:]
    slots = nrow // ngx
    ext = pltpu.VMEM((cx + 2 * H, cy + 2 * HY, nz), jnp.float32)
    rowbuf = pltpu.VMEM((nrow, cx, nz), jnp.float32)
    vec = pltpu.VMEM((nrow, dpb), jnp.float32)
    nsem = 16 + (ngrp * ngx - 1) + (ngy - 1) + 2 * (ngx - 1)
    grid = jax.ShapeDtypeStruct((cx, cy, nz), jnp.float32)
    vm = pl.BlockSpec(memory_space=pltpu.VMEM)
    sm = pl.BlockSpec(memory_space=pltpu.SMEM)
    outs = pl.pallas_call(
        functools.partial(kernel, ngrp, ngx, ngy, slots),
        out_shape=(grid,) * 5 + (jax.ShapeDtypeStruct((nrow, dpb), jnp.float32),),
        in_specs=[vm] * 5 + [sm] + [vm] * 4,
        out_specs=(vm,) * 6,
        scratch_shapes=[
            ext, ext, ext, ext, ext, ext, ext, ext, ext,
            pltpu.VMEM((2, cx, 16, nz), jnp.float32),
            pltpu.VMEM((2, cx + 2 * H, 16, nz), jnp.float32),
            pltpu.VMEM((8, nz), jnp.float32),
            pltpu.VMEM((ngrp * ngx - 1, 8, nz), jnp.float32),
            pltpu.VMEM((8, nz), jnp.float32),
            pltpu.VMEM((ngy - 1, 8, nz), jnp.float32),
            pltpu.VMEM((NBD, cx, nz), jnp.float32),
            rowbuf, rowbuf, vec, vec, rowbuf, rowbuf,
            pltpu.VMEM((NBD, cx, nz), jnp.float32),
            pltpu.VMEM((cx, cy, nz), jnp.float32),
            pltpu.VMEM((cx, cy, nz), jnp.float32),
            pltpu.SemaphoreType.DMA((nsem,)),
            pltpu.SemaphoreType.DMA((nsem,)),
        ],
        compiler_params=pltpu.CompilerParams(collective_id=0, has_side_effects=True),
        name="cloud_step",
    )(
        t, q, u, v, w, owner.reshape(1, -1), count.reshape(nrow, 1),
        size[0, 0], mult[0, 0], cell[0, 0],
    )
    return outs[:5] + (outs[5][None, None],)


def solution(mesh):
    grid = P(("grp", "gx"), "gy", None)
    drop = P(("grp", "gx"), "gy", None, None)
    return jax.shard_map(
        functools.partial(on_device, mesh.shape["grp"], mesh.shape["gx"], mesh.shape["gy"]),
        mesh=mesh,
        in_specs=(grid,) * 7 + (drop,) * 3,
        out_specs=(grid,) * 5 + (drop,),
        check_vma=False,
    )
```

time: 448 us -> 72.2 us (0.16)
  blocking collectives: 149 us -> 0 us
  local copies, waits for them, and re-layouts: 109 us -> 7.34 us
  other arithmetic: 69.3 us -> 0 us
  Pallas kernels: 0 us -> 63.9 us
  waiting for transfers between devices: 61.6 us -> 0 us
  starting transfers between devices: 40.9 us -> 0 us
  between operations: 15.2 us -> 0.66 us
    psum x4 -> x0, blocking collectives: 149 us -> none  [both_sums(): lax.psum((jnp.sum(residual * residual), jnp.sum(residual * applied)), ('g...]
    gather x4 -> x0, local copies, waits for them, and re-layouts: 100 us -> none  [the longest x2 50.1 us: grow_rows(): warmth = jnp.take_along_axis(thermal_couple[:, 1], local_cell, axis=1)]
    pallas_call x0 -> x1, Pallas kernels: none -> 63.9 us  [on_device(): pl.pallas_call(functools.partial(kernel, ngrp, ngx, ngy, slots), out_shap...]
    scatter-add x1 -> x0, other arithmetic: 56.7 us -> none  [grow_rows(): jax.ops.segment_sum(mass_change.reshape(-1), flat_cell.reshape(-1), num_s...]
    ppermute x28 -> x0, waiting for transfers between devices: 42.7 us -> none  [the longest x14 33.7 us: with_halo(): lax.ppermute(lax.slice_in_dim(block, block.shape[dim] - width, None, axis...]
    ppermute x28 -> x0, starting transfers between devices: 33.6 us -> none  [the longest x14 31.1 us: with_halo(): lax.ppermute(lax.slice_in_dim(block, 0, width, axis=dim), axis, backward)]
    all_to_all x2 -> x0, waiting for transfers between devices: 18.9 us -> none  [the longest x1 11.6 us: on_device(): lax.all_to_all(columns, 'gx', split_axis=0, concat_axis=0, tiled=True)]
    all_to_all x2 -> x0, starting transfers between devices: 7.27 us -> none  [the longest x1 3.77 us: on_device(): lax.all_to_all(columns, 'gx', split_axis=0, concat_axis=0, tiled=True)]
  transfers between devices with their start and end apart: 30 -> 0, of which waited for: 22 -> 0; matrix products, arithmetic and copies ran while one was open for 3% -> 0% of each run, Pallas kernels for 0% -> 0%
where the time goes in v1:
time: 72.2 us; the launch traced here: 71.9 us
  Pallas kernels  63.9 us (89%)
  local copies, waits for them, and re-layouts  7.34 us (10%)
    pallas_call x1, Pallas kernels, on_device(): pl.pallas_call(functools.partial(kernel, ngrp, ngx, ngy, slots), out_shap...  63.9 us
    unnamed x18, local copies, waits for them, and re-layouts  6.67 us

profile of v1, /device:TPU:0, one launch (start us, length us, event | category | flops | bytes accessed | tf_op | source)
XLA Modules:
  0.0 71.9 jit_solution(11724801539418615934)
XLA Ops:
  0.6 0.0 copy-start.5
  0.6 0.6 copy-done.5
  1.3 0.7 copy.16.cnt_ref
  2.0 63.9 %cloud_step.1 = (f32[24,16,128]{2,1,0:T(8,128)}, f32[24,16,128]{2,1,0:T(8,128)}, f32[24,16,128]{2,1,0:T(8,128)}, f32[24,16,128]{2,1,0:T(8,128)}, f32[24,16,128]{2,1,0:T(8,128)}, /*index=5*/f32[8,1024]{1,0:T(8,128)}) custom-call(f32[24,16,128]{2,1,0:T(8,128)} %t_ref.1, f32[24,16,128]{2,1,0:T(8,128)} %q_ref.1, f32[24,16,128]{2,1,0:T(8,128)} %u_ref.1, ...), custom_call_target="tpu_custom_call" | custom-call | tf_op jit(solution)/shard_map/cloud_step/pallas_call | solution.py:424
  65.9 0.0 copy-start.3
  65.9 1.7 %copy.23 = f32[24,16,128]{2,1,0:T(8,128)} copy(f32[24,16,128]{2,1,0:T(8,128)} %get-tuple-element.24) | data formatting | bytes 393216
  67.6 0.0 copy-done.3
  67.6 0.0 copy-start.2
  67.6 0.7 copy.24
  68.2 0.3 copy-done.2
  68.6 0.0 copy-start.1
  68.6 0.7 copy.25
  69.2 0.3 copy-done.1
  69.6 0.0 copy-start
  69.6 0.7 copy.26
  70.2 0.3 copy-done
  70.6 0.0 copy-start.4
  70.6 0.7 copy.27
  71.2 0.1 copy-done.4
  71.3 0.6 copy.28
Async XLA Ops:
  0.6 0.7 copy-start.5
  65.9 1.7 %copy-start.3 = (f32[24,16,128]{2,1,0:T(8,128)S(1)}, f32[24,16,128]{2,1,0:T(8,128)}, u32[]{:S(2)}) copy-start(f32[24,16,128]{2,1,0:T(8,128)} %get-tuple-element.25) | copy-start | bytes 589828
  67.6 1.0 %copy-start.2 = (f32[24,16,128]{2,1,0:T(8,128)S(1)}, f32[24,16,128]{2,1,0:T(8,128)}, u32[]{:S(2)}) copy-start(f32[24,16,128]{2,1,0:T(8,128)} %get-tuple-element.26) | copy-start | bytes 589828
  68.6 1.0 %copy-start.1 = (f32[24,16,128]{2,1,0:T(8,128)S(1)}, f32[24,16,128]{2,1,0:T(8,128)}, u32[]{:S(2)}) copy-start(f32[24,16,128]{2,1,0:T(8,128)} %get-tuple-element.27) | copy-start | bytes 589828
  69.6 1.0 %copy-start = (f32[24,16,128]{2,1,0:T(8,128)S(1)}, f32[24,16,128]{2,1,0:T(8,128)}, u32[]{:S(2)}) copy-start(f32[24,16,128]{2,1,0:T(8,128)} %get-tuple-element.28) | copy-start | bytes 589828
  70.6 0.8 %copy-start.4 = (f32[8,1024]{1,0:T(8,128)S(1)}, f32[8,1024]{1,0:T(8,128)}, u32[]{:S(2)}) copy-start(f32[8,1024]{1,0:T(8,128)} %get-tuple-element.17) | copy-start | bytes 98308

commit v2 on v1

--- a/solution.py
+++ b/solution.py
@@ -29,7 +29,19 @@
 H = 5
 HY = 8
 MESH = pl.DeviceIdType.MESH
-HIGH = lax.Precision.HIGHEST
+
+
+def sweep(lo, hi, body, k=8):
+    turns = (hi - lo) // k
+
+    def turn(i, c):
+        for j in range(k):
+            body(lo + i * k + j)
+        return c
+
+    lax.fori_loop(0, turns, turn, 0)
+    for x in range(lo + turns * k, hi):
+        body(x)
 
 
 def cg_coefficients(m):
@@ -78,10 +90,10 @@
 def kernel(
     ngrp, ngx, ngy, slots,
     t_ref, q_ref, u_ref, v_ref, w_ref, map_ref, cnt_ref, size_ref, mult_ref, cell_ref,
-    to_ref, qo_ref, uo_ref, vo_ref, wo_ref, so_ref,
-    ue, ve, le, te, qe, p0, p1, p2, p3, pack, got, part, got_x, part2, got_y,
-    blk, out1, in1, sat_s, tmp_s, out2, in2, cond, grid_c, packed,
-    send_sem, recv_sem,
+    to_ref, qo_ref, uo_ref, vo_ref, wo_ref, so_ref, cond,
+    ue, ve, le, te, qe, p0, p1, p2, p3, phi_s, pack, got, part, got_x,
+    blk, out1, in1, sat_s, tmp_s, live_s, lev_s, hot_s, out2, in2, packed,
+    send_sem, recv_sem, sum_send, sum_recv,
 ):
     cx, cy, nz = t_ref.shape
     rows = 2 * HY + cy
@@ -94,15 +106,20 @@
         return (lax.div(other, ngx), lax.rem(other, ngx), lax.rem(gy + dy + ngy, ngy))
 
     barrier = pltpu.get_barrier_semaphore()
-    greet = [dev(o, 0) for o in range(1, nx)] + [dev(0, o) for o in range(1, ngy)]
-    greet += [dev(a, b) for a in (-1, 1) for b in (-1, 1)]
-    greet += []
-    for target in greet:
-        pl.semaphore_signal(barrier, inc=1, device_id=target, device_id_type=MESH)
+    everyone = nx * ngy
+
+    def other(o):
+        return dev(lax.div(o, ngy), lax.rem(o, ngy))
+
+    def greet(o, c):
+        pl.semaphore_signal(barrier, inc=1, device_id=other(o), device_id_type=MESH)
+        return c
+
+    lax.fori_loop(1, everyone, greet, 0)
 
     own = slice(HY, HY + cy)
 
-    def stage(x, c):
+    def stage(x):
         tt, qq, uu, vv = t_ref[x], q_ref[x], u_ref[x], v_ref[x]
         lift = w_ref[x] + DT * (THERMAL_LIFT * tt + HUMID_LIFT * qq)
         ue[x + H, own, :] = uu
@@ -120,10 +137,9 @@
         pack[1, x, 9:13, :] = lift[0:4]
         pack[1, x, 13:14, :] = tt[0:1]
         pack[1, x, 14:15, :] = qq[0:1]
-        return c
-
-    lax.fori_loop(0, cx, stage, 0)
-    pl.semaphore_wait(barrier, len(greet))
+
+    sweep(0, cx, stage)
+    pl.semaphore_wait(barrier, everyone - 1)
 
     sems = [0]
     started = []
@@ -151,8 +167,8 @@
     halo.append(send(pack.at[0], got.at[0, pl.ds(H, cx)], dev(0, 1)))
     halo.append(send(pack.at[1], got.at[1, pl.ds(H, cx)], dev(0, -1)))
     for a, dy in ((0, 1), (1, -1)):
-        halo.append(send(pack.at[a, pl.ds(cx - 5, 5)], got.at[a, pl.ds(0, 5)], dev(1, dy)))
-        halo.append(send(pack.at[a, pl.ds(0, 5)], got.at[a, pl.ds(e, 5)], dev(-1, dy)))
+        halo.append(send(pack.at[a, pl.ds(cx - 4, 4)], got.at[a, pl.ds(1, 4)], dev(1, dy)))
+        halo.append(send(pack.at[a, pl.ds(0, 4)], got.at[a, pl.ds(e, 4)], dev(-1, dy)))
     for src, dst in ((t_ref, te), (q_ref, qe)):
         halo.append(send(src.at[pl.ds(cx - 1, 1)], dst.at[pl.ds(H - 1, 1), own], east))
         halo.append(send(src.at[pl.ds(0, 1)], dst.at[pl.ds(e, 1), own], west))
@@ -176,7 +192,7 @@
     for copy in halo:
         copy.wait_recv()
 
-    def unpack(x, c):
+    def unpack(x):
         s, n = got[0, x], got[1, x]
         ue[x, HY - 4 : HY, :] = s[0:4]
         ve[x, HY - 5 : HY, :] = s[4:9]
@@ -188,18 +204,16 @@
         le[x, HY + cy : HY + cy + 4, :] = n[9:13]
         te[x, HY + cy : HY + cy + 1, :] = n[13:14]
         qe[x, HY + cy : HY + cy + 1, :] = n[14:15]
-        return c
-
-    lax.fori_loop(0, cx + 2 * H, unpack, 0)
-
-    def make_r(x, c):
+
+    sweep(1, cx + 2 * H - 1, unpack)
+
+    def make_r(x):
         vv, ll = ve[x], le[x]
         horiz = (ue[x + 1] - ue[x - 1]) + (pltpu.roll(vv, rows - 1, 0) - pltpu.roll(vv, 1, 0))
         div = rho * (0.5 * horiz) + 0.5 * (rho_up * up(ll) - rho_dn * down(ll))
         p0[x] = div * (-1.0 / DT)
-        return c
-
-    lax.fori_loop(1, cx + 2 * H - 1, make_r, 0)
+
+    sweep(1, cx + 2 * H - 1, make_r)
 
     diag = ((4.0 + HELMHOLTZ) * rho + face + face_dn) / 6.0 - 1.0
     rho6, face6, face_dn6 = rho / 6.0, face / 6.0, face_dn / 6.0
@@ -209,22 +223,19 @@
         side = f[x + 1] + f[x - 1] + pltpu.roll(c, rows - 1, 0) + pltpu.roll(c, 1, 0)
         return diag * c - rho6 * side - face6 * up(c) - face_dn6 * down(c)
 
-    def step1(x, c):
+    def step1(x):
         p1[x] = scaled(p0, x)
-        return c
-
-    def step2(x, c):
+
+    def step2(x):
         p2[x] = 2.0 * scaled(p1, x) - p0[x]
-        return c
-
-    def step3(x, c):
+
+    def step3(x):
         p3[x] = 2.0 * scaled(p2, x) - p1[x]
-        return c
 
     full = cx + 2 * H
-    lax.fori_loop(2, full - 2, step1, 0)
-    lax.fori_loop(3, full - 3, step2, 0)
-    lax.fori_loop(4, full - 4, step3, 0)
+    sweep(2, full - 2, step1)
+    sweep(3, full - 3, step2)
+    sweep(4, full - 4, step3)
 
     def dots(x, acc):
         a0, a1, a2, a3 = p0[x, own, :], p1[x, own, :], p2[x, own, :], p3[x, own, :]
@@ -234,20 +245,50 @@
         pairs = ((a0, a0), (a0, a1), (a1, a1), (a1, a2), (a2, a2), (a2, a3), (a3, a3), (a3, a4))
         return tuple(s + f * g for s, (f, g) in zip(acc, pairs))
 
-    acc = lax.fori_loop(H, e, dots, (jnp.zeros((cy, nz), jnp.float32),) * 8)
-    for i in range(8):
-        part[i : i + 1, :] = jnp.sum(acc[i], axis=0, keepdims=True)
-
-    peers = [send(part, got_x.at[o - 1], dev(o, 0)) for o in range(1, nx)]
+    def dots_two(i, acc):
+        return dots(H + 2 * i + 1, dots(H + 2 * i, acc))
+
+    acc = lax.fori_loop(0, cx // 2, dots_two, (jnp.zeros((cy, nz), jnp.float32),) * 8)
+    if cx % 2:
+        acc = dots(e - 1, acc)
+    corner = lax.broadcasted_iota(jnp.int32, (8, nz), 0) == lax.broadcasted_iota(
+        jnp.int32, (8, nz), 1
+    )
+    sums = jnp.concatenate([jnp.sum(a, axis=0, keepdims=True) for a in acc], axis=0)
+    sums = jnp.sum(sums, axis=1, keepdims=True)
+    part[...] = jnp.sum(jnp.where(corner, sums, 0.0), axis=0, keepdims=True)
+
+    def share(o):
+        return pltpu.make_async_remote_copy(
+            src_ref=part, dst_ref=got_x.at[o - 1],
+            send_sem=sum_send.at[o - 1], recv_sem=sum_recv.at[o - 1],
+            device_id=other(o), device_id_type=MESH,
+        )
+
+    def share_start(o, c):
+        share(o).start()
+        return c
+
+    def share_wait(o, c):
+        share(o).wait()
+        return c
+
+    lax.fori_loop(1, everyone, share_start, 0)
+    dpb = size_ref.shape[1]
+    nrow = ngx * slots
+    nlev = KHI - KLO
+    narrow = lax.broadcasted_iota(jnp.int32, (cx, dpb), 0)
+    place_of = lax.broadcasted_iota(jnp.int32, (1, dpb), 1)
+    for r in range(nrow):
+        cell = cell_ref[r : r + 1, :]
+        hot_s[r] = jnp.where(narrow == cell // (2 * nz), 1.0, 0.0).astype(jnp.bfloat16)
+        lev_s[r : r + 1, :] = (cell // nz) % 2 * nlev + cell % nz - KLO
+        live_s[r : r + 1, :] = jnp.where(place_of < cnt_ref[0, r], 1.0, 0.0)
+    lax.fori_loop(1, everyone, share_wait, 0)
     total = part[...]
-    for o, copy in enumerate(peers):
-        copy.wait_recv()
+    for o in range(everyone - 1):
         total = total + got_x[o]
-    part2[...] = total
-    peers = [send(part2, got_y.at[o - 1], dev(0, o)) for o in range(1, ngy)]
-    for o, copy in enumerate(peers):
-        copy.wait_recv()
-        total = total + got_y[o]
+    total = jnp.where(corner, total, 0.0)
     total = jnp.broadcast_to(jnp.sum(total, axis=1, keepdims=True), (8, nz))
     dot = [total[i : i + 1, :] for i in range(8)]
     m = [dot[0], dot[1]]
@@ -255,24 +296,22 @@
         m.append(2.0 * dot[k] - m[k % 2])
     c0, c1, c2, c3 = cg_coefficients(m)
 
-    def potential(x, c):
-        p0[x] = c0 * p0[x] + c1 * p1[x] + c2 * p2[x] + c3 * p3[x]
-        return c
-
-    lax.fori_loop(H - 1, e + 1, potential, 0)
+    def potential(x):
+        phi_s[x] = c0 * p0[x] + c1 * p1[x] + c2 * p2[x] + c3 * p3[x]
+
+    sweep(H - 1, e + 1, potential)
 
     sub = lax.broadcasted_iota(jnp.int32, (cy, nz), 0)
     lanes = lax.broadcasted_iota(jnp.int32, (cy, nz), 1)
-    nlev = KHI - KLO
-    half = 2 * nlev
+    half = nz // 2
     south = slice(HY - 1, HY + cy - 1)
     north = slice(HY + 1, HY + cy + 1)
 
-    def advance(x, c):
+    def advance(x):
         g = x + H
-        phi = p0[g, own, :]
-        u = ue[g, own, :] - (DT * 0.5) * (p0[g + 1, own, :] - p0[g - 1, own, :])
-        v = ve[g, own, :] - (DT * 0.5) * (p0[g, north, :] - p0[g, south, :])
+        phi = phi_s[g, own, :]
+        u = ue[g, own, :] - (DT * 0.5) * (phi_s[g + 1, own, :] - phi_s[g - 1, own, :])
+        v = ve[g, own, :] - (DT * 0.5) * (phi_s[g, north, :] - phi_s[g, south, :])
         w = le[g, own, :] - (DT * 0.5) * (not_top * up(phi) - not_bot * down(phi))
         uo_ref[x] = u
         vo_ref[x] = v
@@ -297,18 +336,16 @@
         qo_ref[x] = qq
         sat = qq * jnp.exp(-CLAUSIUS_FACTOR * tt) - 1.0
         both = jnp.where(
-            lanes < nlev, pltpu.roll(sat, nz - KLO, 1), pltpu.roll(tt, nz - KLO + nlev, 1)
+            lanes < half, pltpu.roll(sat, nz - KLO, 1), pltpu.roll(tt, nz - KLO + half, 1)
         )
-        odd = pltpu.roll(pltpu.roll(both, cy - 1, 0), half, 1)
-        packed[x] = jnp.where(lanes < half, both, odd)
-        return c
-
-    lax.fori_loop(0, cx, advance, 0)
+        odd = pltpu.roll(pltpu.roll(both, cy - 1, 0), nlev, 1)
+        packed[x] = jnp.where(lanes % half < nlev, both, odd)
+
+    sweep(0, cx, advance)
     for x in range(cx):
         for b in range(NBD):
             blk[b, x : x + 1, :] = packed[x, 2 * b : 2 * b + 1, :]
 
-    nrow = ngx * slots
     for r in range(nrow):
         o, t = r // slots, r % slots
         row = None
@@ -335,26 +372,19 @@
 
     exchange(out1, in1)
 
-    dpb = size_ref.shape[1]
-    wide = lax.broadcasted_iota(jnp.int32, (nz, dpb), 0)
-    narrow = lax.broadcasted_iota(jnp.int32, (cx, dpb), 0)
-
-    def place(r):
-        cell = cell_ref[pl.ds(r, 1), :]
-        lx = cell // (2 * nz)
-        s = (cell // nz) % 2 * half + cell % nz - KLO
-        return jnp.where(narrow == lx, 1.0, 0.0), s
-
+    wide = lax.broadcasted_iota(jnp.int32, (half, dpb), 0)
+    flip = (((0,), (0,)), ((), ()))
+    f32 = jnp.float32
     for r in range(nrow):
-        hot, s = place(r)
-        res = lax.dot_general(
-            in1[r], hot, (((0,), (0,)), ((), ())), precision=HIGH,
-            preferred_element_type=jnp.float32,
-        )
-        sat_s[r : r + 1, :] = jnp.sum(jnp.where(wide == s, res, 0.0), axis=0, keepdims=True)
-        tmp_s[r : r + 1, :] = jnp.sum(
-            jnp.where(wide == s + nlev, res, 0.0), axis=0, keepdims=True
-        )
+        table, hot = in1[r], hot_s[r]
+        big = table.astype(jnp.bfloat16)
+        rest = table - big.astype(f32)
+        mid = rest.astype(jnp.bfloat16)
+        res = lax.dot_general(big, hot, flip, preferred_element_type=f32)
+        res = res + lax.dot_general(mid, hot, flip, preferred_element_type=f32)
+        mask = wide == lev_s[r : r + 1, :]
+        sat_s[r : r + 1, :] = jnp.sum(jnp.where(mask, res[:half], 0.0), axis=0, keepdims=True)
+        tmp_s[r : r + 1, :] = jnp.sum(jnp.where(mask, res[half:], 0.0), axis=0, keepdims=True)
 
     rate = (2.0 * SUB_STEP * GROWTH) * jnp.exp(GROWTH_SLOPE * tmp_s[...])
     gain = rate * sat_s[...]
@@ -363,7 +393,7 @@
     x2 = old
     for _ in range(NSUB):
         x2 = jnp.maximum(x2 + gain - loss * lax.rsqrt(x2), FLOOR_SQUARE)
-    alive = lax.broadcasted_iota(jnp.int32, (nrow, dpb), 1) < cnt_ref[...]
+    alive = live_s[...] > 0.5
     new = jnp.where(alive, x2, old)
     so_ref[...] = new
     sat_s[...] = jnp.where(
@@ -372,13 +402,16 @@
         0.0,
     )
 
+    across = (((1,), (1,)), ((), ()))
     for r in range(nrow):
-        hot, s = place(r)
-        mass = jnp.where(wide == s, sat_s[r : r + 1, :], 0.0)
-        out2[r] = lax.dot_general(
-            hot, mass, (((1,), (1,)), ((), ())), precision=HIGH,
-            preferred_element_type=jnp.float32,
-        )
+        mass = sat_s[r : r + 1, :]
+        big = mass.astype(jnp.bfloat16).astype(f32)
+        mask = wide == lev_s[r : r + 1, :]
+        hi = jnp.where(mask, big, 0.0).astype(jnp.bfloat16)
+        lo = jnp.where(mask, mass - big, 0.0).astype(jnp.bfloat16)
+        both = jnp.concatenate([hi, lo], axis=0)
+        res = lax.dot_general(hot_s[r], both, across, preferred_element_type=f32)
+        out2[r] = res + pltpu.roll(res, half, 1)
 
     exchange(out2, in2)
 
@@ -388,26 +421,34 @@
             term = jnp.where(map_ref[0, b] == o, 1.0, 0.0) * in2[o * slots + b % slots]
             acc = term if acc is None else acc + term
         cond[b] = acc
+    for copy in started:
+        copy.wait_send()
+
+
+def finish(t_ref, q_ref, u_ref, v_ref, w_ref, s_ref, cond, to, qo, uo, vo, wo, so, grid_c):
+    cx, cy, nz = t_ref.shape
+    nlev = KHI - KLO
+    uo[...] = u_ref[...]
+    vo[...] = v_ref[...]
+    wo[...] = w_ref[...]
+    so[...] = s_ref[...]
     for x in range(cx):
         for b in range(NBD):
             line = cond[b, x : x + 1, :]
             grid_c[x, 2 * b : 2 * b + 1, :] = line
             grid_c[x, 2 * b + 1 : 2 * b + 2, :] = line
-
-    even = sub % 2 == 0
+    even = lax.broadcasted_iota(jnp.int32, (cy, nz), 0) % 2 == 0
+    lanes = lax.broadcasted_iota(jnp.int32, (cy, nz), 1)
     inside = (lanes >= KLO) & (lanes < KHI)
 
-    def finish(x, c):
+    def column(x):
         f = grid_c[x]
-        f = jnp.where(even, pltpu.roll(f, KLO, 1), pltpu.roll(f, nz + KLO - half, 1))
+        f = jnp.where(even, pltpu.roll(f, KLO, 1), pltpu.roll(f, KLO - nlev, 1))
         f = jnp.where(inside, f, 0.0)
-        to_ref[x] = to_ref[x] + PHASE_WARMING * f
-        qo_ref[x] = qo_ref[x] - f
-        return c
-
-    lax.fori_loop(0, cx, finish, 0)
-    for copy in started:
-        copy.wait_send()
+        to[x] = t_ref[x] + PHASE_WARMING * f
+        qo[x] = q_ref[x] - f
+
+    sweep(0, cx, column, 4)
 
 
 def on_device(ngrp, ngx, ngy, t, q, u, v, w, owner, count, size, mult, cell):
@@ -417,37 +458,49 @@
     ext = pltpu.VMEM((cx + 2 * H, cy + 2 * HY, nz), jnp.float32)
     rowbuf = pltpu.VMEM((nrow, cx, nz), jnp.float32)
     vec = pltpu.VMEM((nrow, dpb), jnp.float32)
-    nsem = 16 + (ngrp * ngx - 1) + (ngy - 1) + 2 * (ngx - 1)
+    nsem = 16 + 2 * (ngx - 1)
+    nsum = ngrp * ngx * ngy - 1
     grid = jax.ShapeDtypeStruct((cx, cy, nz), jnp.float32)
     vm = pl.BlockSpec(memory_space=pltpu.VMEM)
     sm = pl.BlockSpec(memory_space=pltpu.SMEM)
-    outs = pl.pallas_call(
+    flat = jax.ShapeDtypeStruct((nrow, dpb), jnp.float32)
+    blocks = jax.ShapeDtypeStruct((NBD, cx, nz), jnp.float32)
+    mid = pl.pallas_call(
         functools.partial(kernel, ngrp, ngx, ngy, slots),
-        out_shape=(grid,) * 5 + (jax.ShapeDtypeStruct((nrow, dpb), jnp.float32),),
-        in_specs=[vm] * 5 + [sm] + [vm] * 4,
-        out_specs=(vm,) * 6,
+        out_shape=(grid,) * 5 + (flat, blocks),
+        in_specs=[vm] * 5 + [sm] * 2 + [vm] * 3,
+        out_specs=(vm,) * 7,
         scratch_shapes=[
-            ext, ext, ext, ext, ext, ext, ext, ext, ext,
+            ext, ext, ext, ext, ext, ext, ext, ext, ext, ext,
             pltpu.VMEM((2, cx, 16, nz), jnp.float32),
             pltpu.VMEM((2, cx + 2 * H, 16, nz), jnp.float32),
-            pltpu.VMEM((8, nz), jnp.float32),
-            pltpu.VMEM((ngrp * ngx - 1, 8, nz), jnp.float32),
-            pltpu.VMEM((8, nz), jnp.float32),
-            pltpu.VMEM((ngy - 1, 8, nz), jnp.float32),
+            pltpu.VMEM((1, nz), jnp.float32),
+            pltpu.VMEM((nsum, 1, nz), jnp.float32),
             pltpu.VMEM((NBD, cx, nz), jnp.float32),
-            rowbuf, rowbuf, vec, vec, rowbuf, rowbuf,
-            pltpu.VMEM((NBD, cx, nz), jnp.float32),
-            pltpu.VMEM((cx, cy, nz), jnp.float32),
+            rowbuf, rowbuf, vec, vec, vec,
+            pltpu.VMEM((nrow, dpb), jnp.int32),
+            pltpu.VMEM((nrow, cx, dpb), jnp.bfloat16),
+            rowbuf, rowbuf,
             pltpu.VMEM((cx, cy, nz), jnp.float32),
             pltpu.SemaphoreType.DMA((nsem,)),
             pltpu.SemaphoreType.DMA((nsem,)),
+            pltpu.SemaphoreType.DMA((nsum,)),
+            pltpu.SemaphoreType.DMA((nsum,)),
         ],
         compiler_params=pltpu.CompilerParams(collective_id=0, has_side_effects=True),
         name="cloud_step",
     )(
-        t, q, u, v, w, owner.reshape(1, -1), count.reshape(nrow, 1),
+        t, q, u, v, w, owner.reshape(1, -1), count.reshape(1, -1),
         size[0, 0], mult[0, 0], cell[0, 0],
     )
+    outs = pl.pallas_call(
+        finish,
+        out_shape=(grid,) * 5 + (flat,),
+        in_specs=[vm] * 7,
+        out_specs=(vm,) * 6,
+        scratch_shapes=[pltpu.VMEM((cx, cy, nz), jnp.float32)],
+        name="finish",
+    )(*mid)
     return outs[:5] + (outs[5][None, None],)
 
 

time: 72.2 us -> 44.7 us (0.62)
  Pallas kernels: 63.9 us -> 43.8 us
  local copies, waits for them, and re-layouts: 7.34 us -> 0 us
    pallas_call x1, Pallas kernels: 63.9 us -> 41 us  [on_device(): pl.pallas_call(functools.partial(kernel, ngrp, ngx, ngy, slots), out_shap...]
    unnamed x18 -> x0, local copies, waits for them, and re-layouts: 6.67 us -> none
    pallas_call x0 -> x1, Pallas kernels: none -> 2.86 us  [on_device(): pl.pallas_call(finish, out_shape=(grid,) * 5 + (flat,), in_specs=[vm] * 7...]
where the time goes in v2:
time: 44.7 us; the launch traced here: 44.5 us
  Pallas kernels  43.8 us (98%)
  between operations  0.64 us (1%)
    pallas_call x1, Pallas kernels, on_device(): pl.pallas_call(functools.partial(kernel, ngrp, ngx, ngy, slots), out_shap...  41 us
    pallas_call x1, Pallas kernels, on_device(): pl.pallas_call(finish, out_shape=(grid,) * 5 + (flat,), in_specs=[vm] * 7...  2.86 us

profile of v2, /device:TPU:0, one launch (start us, length us, event | category | flops | bytes accessed | tf_op | source)
XLA Modules:
  0.0 44.5 jit_solution(14967120122827944596)
XLA Ops:
  0.6 41.0 %cloud_step.1 = (f32[24,16,128]{2,1,0:T(8,128)}, f32[24,16,128]{2,1,0:T(8,128)}, f32[24,16,128]{2,1,0:T(8,128)}, f32[24,16,128]{2,1,0:T(8,128)}, f32[24,16,128]{...) custom-call(f32[24,16,128]{2,1,0:T(8,128)} %t_ref.1, f32[24,16,128]{2,1,0:T(8,128)} %q_ref.1, ...), custom_call_target="tpu_custom_call" | custom-call | tf_op jit(solution)/shard_map/cloud_step/pallas_call | solution.py:468
  41.6 2.9 %finish.1 = (f32[24,16,128]{2,1,0:T(8,128)}, f32[24,16,128]{2,1,0:T(8,128)}, f32[24,16,128]{2,1,0:T(8,128)}, f32[24,16,128]{2,1,0:T(8,128)}, f32[24,16,128]{2,1,0:T(8,128)}, /*index=5*/f32[8,1024]{1,0:T(8,128)}) custom-call(f32[24,16,128]{2,1,0:T(8,128)} %get-tuple-element.19.t_ref, f32[24,16,128]{2,1,0:T(8,128)} %get-tuple-element.20.q_ref, ...), custom_call_target="tpu_custom_call" | custom-call | tf_op jit(solution)/shard_map/finish/pallas_call | solution.py:496
